TPU v7x, 256 devices: a whole 4x4x8 slice. The times are simulated.
256 devices in a mesh: space: 32 (over y, z_hi, core), band: 8 (over x, z_lo).
Axes of the slice: x: 4, y: 4, z: 8 (z_hi: 4, z_lo: 2; z = z_hi * 2 + z_lo), core: 2. Of those that a mesh axis runs over, the one named last changes fastest.
Arguments:
- orbitals: float32 [320, 128, 512], P('band', 'space'), may hold values from -6 to 6
- potential: float32 [128, 512], P('space'), may hold values from -2 to 0
- rotation: float32 [320, 320], replicated, may hold values from -0.3125 to 0.3125
Outputs:
- rotated: float32 [320, 128, 512], P('band', 'space')
All inputs are finite; a program needn't handle non-finite values.
Results may differ from a plain program's by a relative error of at most 0.00007.
Values sent between devices are 32-bit elements; how exact they have to be, the bound alone decides.
No kernel may reach another device: no remote copies, remote signals or barrier semaphores. Data moves between devices by JAX's collectives and lax.ppermute only.
A program may use at most 64 MiB of HBM per device.

v0:
```python
import jax
import jax.numpy as jnp
import numpy as np
from jax import lax
from jax.experimental import pallas as pl
from jax.experimental.pallas import tpu as pltpu
from jax.sharding import Mesh
from jax.sharding import PartitionSpec as P

DEG = 4
NY = 16
NZ = 32
PLANE = NY * NZ
NORB = 320
BAND = ("x", "zl")
SPACE = ("y", "zh", "core")

coef_lap = (-205.0 / 72.0, 8.0 / 5.0, -1.0 / 5.0, 8.0 / 315.0, -1.0 / 560.0)
center_val = 6.0
half_width = 4.0
SCALE = -0.5 / half_width


def lateral():
    def ring(n):
        m = np.zeros((n, n))
        for k in range(1, 5):
            for i in range(n):
                m[i, (i + k) % n] += coef_lap[k]
                m[i, (i - k) % n] += coef_lap[k]
        return m

    lap = np.kron(np.eye(NY), ring(NZ)) + np.kron(ring(NY), np.eye(NZ))
    lap += 3.0 * coef_lap[0] * np.eye(PLANE)
    full = (SCALE * lap - (center_val / half_width) * np.eye(PLANE)).astype(np.float32)
    high = full.astype(jnp.bfloat16)
    low = (full - high.astype(np.float32)).astype(jnp.bfloat16)
    return high, low


def split(v):
    high = v.astype(jnp.bfloat16)
    low = (v - high.astype(jnp.float32)).astype(jnp.bfloat16)
    return high, low


def filter_kernel(mine_ref, low_ref, high_ref, mh_ref, ml_ref, out_ref, pot_ref, *bufs):
    core = lax.axis_index("core")
    at = 0
    for ref in (low_ref, mine_ref, high_ref):
        for zh in range(ref.shape[0]):
            for s in range(2):
                for q in range(6):
                    for j in range(4):
                        piece = ref[zh, s, q, :, j * 128 : (j + 1) * 128]
                        if q < 5:
                            bufs[0][q, j, at : at + 4, :] = piece
                        else:
                            pot_ref[j, at : at + 4, :] = piece * (1.0 / half_width)
                at += 4
    for step in range(1, DEG + 1):
        rows = 64 - 8 * step
        cur, nxt = bufs[step - 1], bufs[step]
        lanes = [cur[:, j, 4 : 4 + rows, :].reshape(5 * rows, 128) for j in range(4)]
        field = jnp.concatenate(lanes, axis=1)
        high, low = split(field)
        dot = lambda a, b: jnp.dot(a, b, preferred_element_type=jnp.float32)
        lat = dot(high, mh_ref[...]) + (dot(low, mh_ref[...]) + dot(high, ml_ref[...]))
        for q in range(5):
            for j in range(4):
                acc = lat[q * rows : (q + 1) * rows, j * 128 : (j + 1) * 128]
                center = cur[q, j, 4 : 4 + rows, :]
                acc = acc + pot_ref[j, 4 * step : 4 * step + rows, :] * center
                for k in range(1, 5):
                    acc = acc + (SCALE * coef_lap[k]) * (
                        cur[q, j, 4 + k : 4 + k + rows, :] + cur[q, j, 4 - k : 4 - k + rows, :]
                    )
                if step > 1:
                    acc = 2.0 * acc - bufs[step - 2][q, j, 8 : 8 + rows, :]
                if step < DEG:
                    nxt[q, j, 0:rows, :] = acc
                else:
                    half, tile = divmod(j, 2)
                    for zh in range(4):
                        for s in range(2):
                            row = (half * 4 + zh) * 10 + q * 2 + tile
                            at = zh * 8 + s * 4
                            out_ref[s ^ core, pl.ds(row, 4, stride=80), :] = acc[at : at + 4, :]


def run_filter(mine, low, high):
    mh, ml = lateral()
    vmem = pl.BlockSpec(memory_space=pltpu.VMEM)
    return pl.pallas_call(
        filter_kernel,
        out_shape=jax.ShapeDtypeStruct((2, 320, 128), jnp.float32),
        in_specs=[vmem] * 5,
        out_specs=vmem,
        scratch_shapes=[pltpu.VMEM((4, 64, 128), jnp.float32)]
        + [pltpu.VMEM((5, 4, 64 - 8 * s, 128), jnp.float32) for s in range(DEG)]
        + [pltpu.VMEM((8, 128), jnp.float32)],
        compiler_params=pltpu.CompilerParams(vmem_limit_bytes=24 << 20),
        name="filter",
    )(mine, low, high, jnp.asarray(mh), jnp.asarray(ml))


def rotate_kernel(weights_ref, field_ref, out_ref):
    field = jnp.concatenate(
        [field_ref[pl.ds(tile, NORB, stride=2), :] for tile in range(2)], axis=1
    )
    out_ref[...] = jnp.dot(
        weights_ref[...],
        field,
        precision=lax.Precision.HIGHEST,
        preferred_element_type=jnp.float32,
    )


def run_rotate(weights, field):
    vmem = pl.BlockSpec(memory_space=pltpu.VMEM)
    return pl.pallas_call(
        rotate_kernel,
        out_shape=jax.ShapeDtypeStruct((NORB, 256), jnp.float32),
        in_specs=[vmem] * 2,
        out_specs=vmem,
        compiler_params=pltpu.CompilerParams(vmem_limit_bytes=8 << 20),
        name="rotate",
    )(weights, field)


SWAP = [(0, 1), (1, 0)]
UP = [(0, 1), (1, 2), (2, 3), (3, 0)]
DOWN = [(1, 0), (2, 1), (3, 2), (0, 3)]


def local(orbitals, potential, rotation):
    core = lax.axis_index("core")
    pairs = orbitals.reshape(20, 2, 4, PLANE)
    give = lax.dynamic_index_in_dim(pairs, 1 - core, 1, keepdims=False)
    keep = lax.dynamic_index_in_dim(pairs, core, 1, keepdims=False)
    give = jnp.concatenate([give, potential[None]], axis=0)
    got = lax.ppermute(give, "core", SWAP)

    def six(block, pot):
        block = block.reshape(4, 5, 4, PLANE)
        return jnp.concatenate(
            [block, jnp.broadcast_to(pot[None, None], (4, 1, 4, PLANE))], axis=1
        )

    own = six(keep, potential)
    other = six(got[:20], got[20])
    payload = jnp.where(
        core == 0,
        jnp.stack([own, other], axis=1),
        jnp.stack([other, own], axis=1),
    )
    mine = lax.all_to_all(payload, "zh", 0, 0, tiled=True)
    low = lax.ppermute(mine[2:4], "y", UP)
    high = lax.ppermute(mine[0:2], "y", DOWN)
    halves = run_filter(mine, low, high)
    got = lax.ppermute(halves[1], "core", SWAP)
    own = halves[0].reshape(32, 5, 1, 2, 128)
    other = got.reshape(32, 5, 1, 2, 128)
    payload = jnp.where(
        core == 0,
        jnp.concatenate([own, other], axis=2),
        jnp.concatenate([other, own], axis=2),
    )
    columns = lax.all_to_all(payload.reshape(32, 5, 4, 128), BAND + ("zh",), 0, 0, tiled=True)
    turned = run_rotate(rotation.T, columns.reshape(640, 128))
    back = lax.all_to_all(turned.reshape(8, 40, 256), BAND, 0, 0, tiled=True)
    return back.reshape(4, 2, 40, 256).transpose(2, 0, 1, 3).reshape(40, 4, PLANE)


def solution(mesh):
    fine = Mesh(mesh.devices.reshape(4, 4, 2, 4, 2), SPACE + BAND)
    placed = (P(BAND, SPACE, None), P(SPACE, None), P())
    return jax.shard_map(
        local, mesh=fine, in_specs=placed, out_specs=P(BAND, SPACE, None), check_vma=False
    )
```

profile of v0, /device:TPU:2, one launch (start us, length us, event | category | flops | bytes accessed | tf_op | source)
XLA Modules:
  0.0 72.5 jit_solution(2094953246805991360)
XLA Ops:
  0.0 0.0 copy-start.3
  0.0 1.0 %constant_dynamic-slice_fusion = (f32[20,1,4,512]{3,2,1,0:T(4,128)S(1)}, f32[20,4,512]{2,1,0:T(4,128)S(1)}) fusion(f32[20,2,4,512]{3,2,1,0:T(4,128)} %bitcast.34, s32[]{:T(128)S(6)} %select_n.29, s32[]{:T(128)S(6)} %select_n.30), kind=kLoop, calls=%fused_computation.9 | loop fusion | bytes 655368 | tf_op jit(solution)/shard_map/jit(dynamic_index_in_dim)/dynamic_slice | solution.py:140
  1.0 0.0 copy-done.3
  1.1 0.1 collective-permute-start
  1.3 1.3 %collective-permute-done = f32[21,4,512]{2,1,0:T(4,128)S(1)} collective-permute-done((f32[21,4,512]{2,1,0:T(4,128)S(1)}, f32[21,4,512]{2,1,0:T(4,128)S(1)}, u32[]{:S(2)}, u32[]{:S(2)}) %collective-permute-start) | collective-permute-done | bytes 172064 | tf_op jit(solution)/shard_map/ppermute | solution.py:142
  2.7 0.1 maximum_select_fusion
  2.8 0.0 copy-start.1
  2.8 22.5 %all_to_all.15.mine_ref = f32[4,2,6,4,512]{4,3,2,1,0:T(4,128)S(1)} all-to-all(f32[4,2,6,4,512]{4,3,2,1,0:T(4,128)S(1)} %maximum_select_fusion), channel_id=1, replica_groups=mesh['y'=4,'zh'=4,'core'=2,'x'=4,'zl'=2] {'zh'}, dimensions={0} | all-to-all | bytes 786432 | tf_op jit(solution)/shard_map/all_to_all | solution.py:157
  25.3 0.0 copy-start
  25.4 3.1 %collective-permute-start.2 = (f32[2,2,6,4,512]{4,3,2,1,0:T(4,128)S(1)}, f32[2,2,6,4,512]{4,3,2,1,0:T(4,128)S(1)}, u32[]{:S(2)}, u32[]{:S(2)}) collective-permute-start(f32[2,2,6,4,512]{4,3,2,1,0:T(4,128)S(1)} %get-tuple-element.5), channel_id=1, source_target_pairs={{64,0},{128,64},{192,128},{0,192},{65,1},{129,65},{193,129},{1,193... | collective-permute-start | bytes 589832 | tf_op jit(solution)/shard_map/ppermute | solution.py:159
  28.5 0.0 collective-permute-start.1
  28.5 3.2 %collective-permute-done.2.high_ref = f32[2,2,6,4,512]{4,3,2,1,0:T(4,128)S(1)} collective-permute-done((f32[2,2,6,4,512]{4,3,2,1,0:T(4,128)S(1)}, f32[2,2,6,4,512]{4,3,2,1,0:T(4,128)S(1)}, u32[]{:S(2)}, u32[]{:S(2)}) %collective-permute-start.2) | collective-permute-done | bytes 196640 | tf_op jit(solution)/shard_map/ppermute | solution.py:159
  31.6 3.7 %collective-permute-done.1.low_ref = f32[2,2,6,4,512]{4,3,2,1,0:T(4,128)S(1)} collective-permute-done((f32[2,2,6,4,512]{4,3,2,1,0:T(4,128)S(1)}, f32[2,2,6,4,512]{4,3,2,1,0:T(4,128)S(1)}, u32[]{:S(2)}, u32[]{:S(2)}) %collective-permute-start.1) | collective-permute-done | bytes 196640 | tf_op jit(solution)/shard_map/ppermute | solution.py:158
  35.3 0.0 copy-done.1
  35.3 0.0 copy-done
  35.3 2.9 %filter.1 = f32[2,320,128]{2,1,0:T(8,128)S(1)} custom-call(f32[4,2,6,4,512]{4,3,2,1,0:T(4,128)S(1)} %all_to_all.15.mine_ref, f32[2,2,6,4,512]{4,3,2,1,0:T(4,128)S(1)} %collective-permute-done.1.low_ref, f32[2,2,6,4,512]{4,3,2,1,0:T(4,128)S(1)} %collective-permute-done.2.high_ref, bf16[512,512]{1,0:T(8,128)(2,1)S(1)} %copy-done.1, bf16[512,512]{1,0:T(8,128)(2,1)S(1)} %copy-done), custom_call_target="tpu_custom_call" | custom-call | tf_op jit(solution)/shard_map/filter/pallas_call | solution.py:94
  38.3 0.1 collective-permute-start.3
  38.4 1.4 %collective-permute-done.3 = f32[320,128]{1,0:T(8,128)S(1)} collective-permute-done((f32[320,128]{1,0:T(8,128)S(1)}, f32[320,128]{1,0:T(8,128)S(1)}, u32[]{:S(2)}, u32[]{:S(2)}) %collective-permute-start.3) | collective-permute-done | bytes 163872 | tf_op jit(solution)/shard_map/ppermute | solution.py:161
  39.7 0.1 maximum_select_fusion.1
  39.9 0.8 %copy.8 = f32[32,5,2,2,128]{4,3,2,1,0:T(2,128)} copy(f32[32,5,2,2,128]{4,3,1,0,2:T(2,128)S(1)} %maximum_select_fusion.1) | data formatting | bytes 655360 | tf_op jit(solution)/shard_map/jit(_where)/select_n | solution.py:164
  40.7 0.0 copy-start.2
  40.7 6.0 %all-to-all-start.1 = ((f32[32,5,4,128]{3,2,1,0:T(4,128)}), f32[32,5,4,128]{3,2,1,0:T(4,128)S(1)}, u32[]{:S(2)}, u32[]{:S(2)}) async-start(f32[32,5,4,128]{3,2,1,0:T(4,128)} %bitcast.12), calls=%async_computation.1 | async-start | bytes 655360 | tf_op jit(solution)/shard_map/all_to_all | solution.py:169
  46.7 0.0 copy-done.2
  46.7 0.2 copy.6
  46.9 11.8 %all-to-all-done.1 = f32[32,5,4,128]{3,2,1,0:T(4,128)S(1)} async-done(((f32[32,5,4,128]{3,2,1,0:T(4,128)}), f32[32,5,4,128]{3,2,1,0:T(4,128)S(1)}, u32[]{:S(2)}, u32[]{:S(2)}) %all-to-all-start.1) | async-done | bytes 327712 | tf_op jit(solution)/shard_map/all_to_all | solution.py:169
  58.7 0.7 rotate.1
  59.4 11.9 %all_to_all.16 = f32[8,40,256]{2,1,0:T(8,128)S(1)} all-to-all(f32[8,40,256]{2,1,0:T(8,128)S(1)} %bitcast.28), channel_id=1, replica_groups=mesh['y'=4,'zh'=4,'core'=2,'x'=4,'zl'=2] {'x','zl'}, dimensions={0} | all-to-all | bytes 655360 | tf_op jit(solution)/shard_map/all_to_all | solution.py:171
  71.3 0.2 copy.12
  71.5 1.0 %reshape.43 = f32[40,4,512]{2,1,0:T(4,128)} reshape(f32[40,4,2,256]{3,2,1,0:T(2,128)S(1)} %bitcast.30) | data formatting | bytes 655360 | tf_op jit(solution)/shard_map/reshape | solution.py:172
  (9 shorter events, 0.2 us)
Async XLA Ops:
  0.0 1.0 %copy-start.3 = (f32[4,512]{1,0:T(4,128)S(1)}, f32[4,512]{1,0:T(4,128)}, u32[]{:S(2)}) copy-start(f32[4,512]{1,0:T(4,128)} %param.6) | copy-start | bytes 24580
  1.1 1.5 %collective-permute-start = (f32[21,4,512]{2,1,0:T(4,128)S(1)}, f32[21,4,512]{2,1,0:T(4,128)S(1)}, u32[]{:S(2)}, u32[]{:S(2)}) collective-permute-start(f32[21,4,512]{2,1,0:T(4,128)S(1)} %pad_maximum_fusion), channel_id=1, source_target_pairs={{0,8},{8,0},{1,9},{9,1},{2,10},{10,2},{3,11},{11,3},{4,12},{12,4},... | collective-permute-start | bytes 516104 | tf_op jit(solution)/shard_map/ppermute | solution.py:142
  2.8 32.6 %copy-start.1 = (bf16[512,512]{1,0:T(8,128)(2,1)S(1)}, bf16[512,512]{1,0:T(8,128)(2,1)}, u32[]{:S(2)}) copy-start(bf16[512,512]{1,0:T(8,128)(2,1)} %constant.23.clone.mh_ref) | copy-start | bytes 1572868
  25.3 10.0 %copy-start = (bf16[512,512]{1,0:T(8,128)(2,1)S(1)}, bf16[512,512]{1,0:T(8,128)(2,1)}, u32[]{:S(2)}) copy-start(bf16[512,512]{1,0:T(8,128)(2,1)} %constant.24.clone.ml_ref) | copy-start | bytes 1572868
  25.4 6.3 %collective-permute-start.2 = (f32[2,2,6,4,512]{4,3,2,1,0:T(4,128)S(1)}, f32[2,2,6,4,512]{4,3,2,1,0:T(4,128)S(1)}, u32[]{:S(2)}, u32[]{:S(2)}) collective-permute-start(f32[2,2,6,4,512]{4,3,2,1,0:T(4,128)S(1)} %get-tuple-element.5), channel_id=1, source_target_pairs={{64,0},{128,64},{192,128},{0,192},{65,1},{129,65},{193,129},{1,193... | collective-permute-start | bytes 589832 | tf_op jit(solution)/shard_map/ppermute | solution.py:159
  28.5 6.9 %collective-permute-start.1 = (f32[2,2,6,4,512]{4,3,2,1,0:T(4,128)S(1)}, f32[2,2,6,4,512]{4,3,2,1,0:T(4,128)S(1)}, u32[]{:S(2)}, u32[]{:S(2)}) collective-permute-start(f32[2,2,6,4,512]{4,3,2,1,0:T(4,128)S(1)} %get-tuple-element.6), channel_id=1, source_target_pairs={{0,64},{64,128},{128,192},{192,0},{1,65},{65,129},{129,193},{193,1... | collective-permute-start | bytes 589832 | tf_op jit(solution)/shard_map/ppermute | solution.py:158
  38.3 1.5 %collective-permute-start.3 = (f32[320,128]{1,0:T(8,128)S(1)}, f32[320,128]{1,0:T(8,128)S(1)}, u32[]{:S(2)}, u32[]{:S(2)}) collective-permute-start(f32[320,128]{1,0:T(8,128)S(1)} %get-tuple-element.8), channel_id=1, source_target_pairs={{0,8},{8,0},{1,9},{9,1},{2,10},{10,2},{3,11},{11,3},{4,12},{12,4},... | collective-permute-start | bytes 491528 | tf_op jit(solution)/shard_map/ppermute | solution.py:161
  40.7 6.0 %copy-start.2 = (f32[320,320]{1,0:T(8,128)S(1)}, f32[320,320]{1,0:T(8,128)}, u32[]{:S(2)}) copy-start(f32[320,320]{1,0:T(8,128)} %param.7) | copy-start | bytes 1228804
  40.7 18.0 %all-to-all-start.1 = ((f32[32,5,4,128]{3,2,1,0:T(4,128)}), f32[32,5,4,128]{3,2,1,0:T(4,128)S(1)}, u32[]{:S(2)}, u32[]{:S(2)}) async-start(f32[32,5,4,128]{3,2,1,0:T(4,128)} %bitcast.12), calls=%async_computation.1 | async-start | bytes 655360 | tf_op jit(solution)/shard_map/all_to_all | solution.py:169
where the time goes:
time: 72.8 us; the launch traced here: 72.5 us
  blocking collectives  34.5 us (47%)
  waiting for transfers between devices  21.3 us (29%)
  starting transfers between devices  9.26 us (13%)
  Pallas kernels  3.57 us (5%)
  local copies, waits for them, and re-layouts  3.38 us (5%)
    all_to_all x1, blocking collectives, local(): mine = lax.all_to_all(payload, 'zh', 0, 0, tiled=True)  22.5 us
    all_to_all x1, blocking collectives, local(): back = lax.all_to_all(turned.reshape(8, 40, 256), BAND, 0, 0, tiled=True)  11.9 us
    all_to_all x1, waiting for transfers between devices, local(): lax.all_to_all(payload.reshape(32, 5, 4, 128), BAND + ('zh',), 0, 0, tile...  11.8 us
    all_to_all x1, starting transfers between devices, local(): lax.all_to_all(payload.reshape(32, 5, 4, 128), BAND + ('zh',), 0, 0, tile...  5.98 us
    ppermute x1, waiting for transfers between devices, local(): low = lax.ppermute(mine[2:4], 'y', UP)  3.69 us
    ppermute x1, waiting for transfers between devices, local(): high = lax.ppermute(mine[0:2], 'y', DOWN)  3.19 us
    ppermute x1, starting transfers between devices, local(): high = lax.ppermute(mine[0:2], 'y', DOWN)  3.09 us
    pallas_call x1, Pallas kernels, run_filter(): pl.pallas_call(filter_kernel, out_shape=jax.ShapeDtypeStruct((2, 320, 128...  2.88 us
  transfers between devices with their start and end apart: 5, of which 5 were waited for; matrix products, arithmetic and copies ran while one was open for 0% of the time, Pallas kernels for 0%

commit v1 on v0

v1 whole, which is shorter than its diff:
```python
import jax
import jax.numpy as jnp
import numpy as np
from jax import lax
from jax.experimental import pallas as pl
from jax.experimental.pallas import tpu as pltpu
from jax.sharding import Mesh
from jax.sharding import PartitionSpec as P

DEG = 4
NY = 16
NZ = 32
PLANE = NY * NZ
NORB = 320
BAND = ("x", "zl")
SPACE = ("y", "zh", "core")

coef_lap = (-205.0 / 72.0, 8.0 / 5.0, -1.0 / 5.0, 8.0 / 315.0, -1.0 / 560.0)
center_val = 6.0
half_width = 4.0
SCALE = -0.5 / half_width


def lateral():
    def ring(n):
        m = np.zeros((n, n))
        for k in range(1, 5):
            for i in range(n):
                m[i, (i + k) % n] += coef_lap[k]
                m[i, (i - k) % n] += coef_lap[k]
        return m

    lap = np.kron(np.eye(NY), ring(NZ)) + np.kron(ring(NY), np.eye(NZ))
    lap += 3.0 * coef_lap[0] * np.eye(PLANE)
    full = (SCALE * lap - (center_val / half_width) * np.eye(PLANE)).astype(np.float32)
    high = full.astype(jnp.bfloat16)
    low = (full - high.astype(np.float32)).astype(jnp.bfloat16)
    return high, low


def split(v):
    high = v.astype(jnp.bfloat16)
    low = (v - high.astype(jnp.float32)).astype(jnp.bfloat16)
    return high, low


def filter_kernel(*refs):
    pieces, halos = refs[0:4], refs[4:8]
    mh_ref, ml_ref, out_ref, pot_ref = refs[8:12]
    bufs = refs[12:]
    core, zh_here = lax.axis_index("core"), lax.axis_index("zh")
    for ahead in range(4):
        zh = lax.rem(zh_here + (4 - ahead), 4)
        inside = 16 + zh * 8
        outside = jnp.where(zh >= 2, (zh - 2) * 8, 48 + zh * 8)
        for ref, at in ((pieces[ahead], inside), (halos[ahead], outside)):
            rows = pl.ds(pl.multiple_of(at, 8), 8)
            for q in range(6):
                for j in range(4):
                    part = jnp.concatenate(
                        [ref[s, q, :, j * 128 : (j + 1) * 128] for s in range(2)], axis=0
                    )
                    if q < 5:
                        bufs[0][q, j, rows, :] = part
                    else:
                        pot_ref[j, rows, :] = part * (1.0 / half_width)
    for step in range(1, DEG + 1):
        rows = 64 - 8 * step
        cur, nxt = bufs[step - 1], bufs[step % DEG]
        lanes = [cur[:, j, 4 : 4 + rows, :].reshape(5 * rows, 128) for j in range(4)]
        field = jnp.concatenate(lanes, axis=1)
        high, low = split(field)
        dot = lambda a, b: jnp.dot(a, b, preferred_element_type=jnp.float32)
        lat = dot(high, mh_ref[...]) + (dot(low, mh_ref[...]) + dot(high, ml_ref[...]))
        for q in range(5):
            for j in range(4):
                acc = lat[q * rows : (q + 1) * rows, j * 128 : (j + 1) * 128]
                center = cur[q, j, 4 : 4 + rows, :]
                acc = acc + pot_ref[j, 4 * step : 4 * step + rows, :] * center
                for k in range(1, 5):
                    acc = acc + (SCALE * coef_lap[k]) * (
                        cur[q, j, 4 + k : 4 + k + rows, :] + cur[q, j, 4 - k : 4 - k + rows, :]
                    )
                if step > 1:
                    acc = 2.0 * acc - bufs[step - 2][q, j, 8 : 8 + rows, :]
                if step < DEG:
                    nxt[q, j, 0:rows, :] = acc
                    continue
                half, tile = divmod(j, 2)
                for zh in range(4):
                    for s in range(2):
                        row = (half * 4 + zh) * 10 + q * 2 + tile
                        at = zh * 8 + s * 4
                        out_ref[s ^ core, pl.ds(row, 4, stride=80), :] = acc[at : at + 4, :]


def run_filter(pieces, halos):
    mh, ml = lateral()
    vmem = pl.BlockSpec(memory_space=pltpu.VMEM)
    return pl.pallas_call(
        filter_kernel,
        out_shape=jax.ShapeDtypeStruct((2, 320, 128), jnp.float32),
        in_specs=[vmem] * 10,
        out_specs=vmem,
        scratch_shapes=[pltpu.VMEM((4, 64, 128), jnp.float32)]
        + [pltpu.VMEM((5, 4, 64 - 8 * s, 128), jnp.float32) for s in range(DEG)],
        compiler_params=pltpu.CompilerParams(vmem_limit_bytes=24 << 20),
        name="filter",
    )(*pieces, *halos, jnp.asarray(mh), jnp.asarray(ml))


def merge_kernel(kept_ref, got_ref, out_ref):
    core = lax.axis_index("core")
    for side in range(2):

        @pl.when(core == side)
        def _():
            for tile in range(2):
                for slot, ref in ((side, kept_ref), (1 - side, got_ref)):
                    out_ref[pl.ds(slot * 2 + tile, 160, stride=4), :] = ref[
                        pl.ds(tile, 160, stride=2), :
                    ]


def run_merge(kept, got):
    vmem = pl.BlockSpec(memory_space=pltpu.VMEM)
    return pl.pallas_call(
        merge_kernel,
        out_shape=jax.ShapeDtypeStruct((640, 128), jnp.float32),
        in_specs=[vmem] * 2,
        out_specs=vmem,
        compiler_params=pltpu.CompilerParams(vmem_limit_bytes=4 << 20),
        name="merge",
    )(kept, got)


def turn_kernel(weights_ref, high_ref, low_ref):
    high_ref[...], low_ref[...] = split(weights_ref[...].T)


def run_turn(rotation):
    vmem = pl.BlockSpec(memory_space=pltpu.VMEM)
    return pl.pallas_call(
        turn_kernel,
        out_shape=[jax.ShapeDtypeStruct((NORB, NORB), jnp.bfloat16)] * 2,
        in_specs=[vmem],
        out_specs=[vmem] * 2,
        compiler_params=pltpu.CompilerParams(vmem_limit_bytes=8 << 20),
        name="turn",
    )(rotation)


def rotate_kernel(wh_ref, wl_ref, field_ref, out_ref):
    field = jnp.concatenate(
        [field_ref[pl.ds(tile, NORB, stride=2), :] for tile in range(2)], axis=1
    )
    high, low = split(field)
    dot = lambda a, b: jnp.dot(a, b, preferred_element_type=jnp.float32)
    wh = wh_ref[...]
    out_ref[...] = dot(wh, high) + (dot(wh, low) + dot(wl_ref[...], high))


def run_rotate(weights, field):
    vmem = pl.BlockSpec(memory_space=pltpu.VMEM)
    return pl.pallas_call(
        rotate_kernel,
        out_shape=jax.ShapeDtypeStruct((NORB, 256), jnp.float32),
        in_specs=[vmem] * 3,
        out_specs=vmem,
        compiler_params=pltpu.CompilerParams(vmem_limit_bytes=8 << 20),
        name="rotate",
    )(*weights, field)


SWAP = [(0, 1), (1, 0)]


def ahead_by(step):
    return [(zh, (zh + step) % 4) for zh in range(4)]


def outward(ahead):
    pairs = []
    for y in range(4):
        for zh in range(4):
            way = 1 if (zh - ahead) % 4 >= 2 else -1
            pairs.append((y * 4 + zh, (y + way) % 4 * 4 + zh))
    return pairs


def local(orbitals, potential, rotation):
    core, zh_here = lax.axis_index("core"), lax.axis_index("zh")
    pairs = orbitals.reshape(20, 2, 4, PLANE)
    give = lax.dynamic_index_in_dim(pairs, 1 - core, 1, keepdims=False)
    keep = lax.dynamic_index_in_dim(pairs, core, 1, keepdims=False)
    give = jnp.concatenate([give, potential[None]], axis=0)
    got = lax.ppermute(give, "core", SWAP)

    def six(block, pot):
        block = block.reshape(4, 5, 4, PLANE)
        return jnp.concatenate(
            [block, jnp.broadcast_to(pot[None, None], (4, 1, 4, PLANE))], axis=1
        )

    own = six(keep, potential)
    other = six(got[:20], got[20])
    payload = jnp.where(
        core == 0,
        jnp.stack([own, other], axis=1),
        jnp.stack([other, own], axis=1),
    )
    pieces, halos = [None] * 4, [None] * 4
    for ahead in (2, 1, 3, 0):
        piece = lax.dynamic_index_in_dim(payload, (zh_here + ahead) % 4, 0, keepdims=False)
        pieces[ahead] = lax.ppermute(piece, "zh", ahead_by(ahead)) if ahead else piece
    for ahead in (0, 2, 1, 3):
        halos[ahead] = lax.ppermute(pieces[ahead], ("y", "zh"), outward(ahead))
    halves = run_filter(pieces, halos)
    got = lax.ppermute(halves[1], "core", SWAP)
    weights = run_turn(rotation)
    got, weights = lax.optimization_barrier((got, weights))
    merged = run_merge(halves[0], got)
    columns = lax.all_to_all(merged.reshape(32, 5, 4, 128), BAND + ("zh",), 0, 0, tiled=True)
    turned = run_rotate(weights, columns.reshape(640, 128))
    back = lax.all_to_all(turned.reshape(8, 40, 256), BAND, 0, 0, tiled=True)
    return back.reshape(4, 2, 40, 256).transpose(2, 0, 1, 3).reshape(40, 4, PLANE)


def solution(mesh):
    fine = Mesh(mesh.devices.reshape(4, 4, 2, 4, 2), SPACE + BAND)
    placed = (P(BAND, SPACE, None), P(SPACE, None), P())
    return jax.shard_map(
        local, mesh=fine, in_specs=placed, out_specs=P(BAND, SPACE, None), check_vma=False
    )
```

time: 72.8 us -> 66.8 us (0.918)
  waiting for transfers between devices: 21.3 us -> 8.16 us
  starting transfers between devices: 9.26 us -> 19.6 us
  blocking collectives: 34.5 us -> 31.4 us
    ppermute x2 -> x7, starting transfers between devices: 3.09 us -> 19.4 us  [the longest x3 10.2 us: local(): lax.ppermute(piece, 'zh', ahead_by(ahead))]
    all_to_all x1 -> x0, waiting for transfers between devices: 11.8 us -> none  [local(): lax.all_to_all(payload.reshape(32, 5, 4, 128), BAND + ('zh',), 0, 0, tile...]
    all_to_all x1 -> x0, starting transfers between devices: 5.98 us -> none  [local(): lax.all_to_all(payload.reshape(32, 5, 4, 128), BAND + ('zh',), 0, 0, tile...]
    all_to_all x1, blocking collectives: 22.5 us -> 19.5 us  [local(): lax.all_to_all(merged.reshape(32, 5, 4, 128), BAND + ('zh',), 0, 0, tiled...]
    ppermute x1, waiting for transfers between devices: 1.38 us -> 0.27 us  [local(): got = lax.ppermute(halves[1], 'core', SWAP)]
    select_n x1 -> x0, local copies, waits for them, and re-layouts: 0.84 us -> none  [local(): jnp.where(core == 0, jnp.concatenate([own, other], axis=2), jnp.concatena...]
    ppermute x2 -> x7, waiting for transfers between devices: 6.88 us -> 6.63 us  [the longest x4 4.25 us: local(): halos[ahead] = lax.ppermute(pieces[ahead], ('y', 'zh'), outward(ahead))]
  transfers between devices with their start and end apart: 5 -> 9, of which waited for: 5 -> 6; matrix products, arithmetic and copies ran while one was open for 0% -> 0% of each run, Pallas kernels for 0% -> 0%
where the time goes in v1:
time: 66.8 us; the launch traced here: 66.4 us
  blocking collectives  31.4 us (47%)
  starting transfers between devices  19.6 us (29%)
  waiting for transfers between devices  8.16 us (12%)
  Pallas kernels  3.62 us (5%)
  local copies, waits for them, and re-layouts  3.24 us (5%)
    all_to_all x1, blocking collectives, local(): lax.all_to_all(merged.reshape(32, 5, 4, 128), BAND + ('zh',), 0, 0, tiled...  19.5 us
    all_to_all x1, blocking collectives, local(): back = lax.all_to_all(turned.reshape(8, 40, 256), BAND, 0, 0, tiled=True)  11.9 us
    ppermute x3, starting transfers between devices, local(): lax.ppermute(piece, 'zh', ahead_by(ahead))  10.2 us
    ppermute x4, starting transfers between devices, local(): halos[ahead] = lax.ppermute(pieces[ahead], ('y', 'zh'), outward(ahead))  9.18 us
    ppermute x4, waiting for transfers between devices, local(): halos[ahead] = lax.ppermute(pieces[ahead], ('y', 'zh'), outward(ahead))  4.25 us
    pallas_call x1, Pallas kernels, run_filter(): pl.pallas_call(filter_kernel, out_shape=jax.ShapeDtypeStruct((2, 320, 128...  2.96 us
    ppermute x3, waiting for transfers between devices, local(): lax.ppermute(piece, 'zh', ahead_by(ahead))  2.38 us
  transfers between devices with their start and end apart: 9, of which 6 were waited for; matrix products, arithmetic and copies ran while one was open for 0% of the time, Pallas kernels for 0%

profile of v1, /device:TPU:2, one launch (start us, length us, event | category | flops | bytes accessed | tf_op | source)
XLA Modules:
  0.0 66.4 jit_solution(4668779512331860349)
XLA Ops:
  0.0 0.0 copy-start.3
  0.0 1.0 %constant_dynamic-slice_fusion = (f32[20,1,4,512]{3,2,1,0:T(4,128)S(1)}, f32[20,4,512]{2,1,0:T(4,128)S(1)}) fusion(f32[20,2,4,512]{3,2,1,0:T(4,128)} %bitcast.38, s32[]{:T(128)S(6)} %select_n.48, s32[]{:T(128)S(6)} %select_n.49), kind=kLoop, calls=%fused_computation.13 | loop fusion | bytes 655368 | tf_op jit(solution)/shard_map/jit(dynamic_index_in_dim)/dynamic_slice | solution.py:195
  1.0 0.0 copy-done.3
  1.1 0.1 collective-permute-start
  1.3 1.3 %collective-permute-done = f32[21,4,512]{2,1,0:T(4,128)S(1)} collective-permute-done((f32[21,4,512]{2,1,0:T(4,128)S(1)}, f32[21,4,512]{2,1,0:T(4,128)S(1)}, u32[]{:S(2)}, u32[]{:S(2)}) %collective-permute-start) | collective-permute-done | bytes 172064 | tf_op jit(solution)/shard_map/ppermute | solution.py:197
  2.7 0.0 copy-start.1
  2.7 0.1 maximum_select_fusion
  2.8 0.0 copy-start
  2.9 6.4 %collective-permute-start.3 = (f32[2,6,4,512]{3,2,1,0:T(4,128)S(1)}, f32[2,6,4,512]{3,2,1,0:T(4,128)S(1)}, u32[]{:S(2)}, u32[]{:S(2)}) collective-permute-start(f32[2,6,4,512]{3,2,1,0:T(4,128)S(1)} %get-tuple-element.15), channel_id=1, source_target_pairs={{0,48},{16,0},{32,16},{48,32},{1,49},{17,1},{33,17},{49,33},{2,50}... | collective-permute-start | bytes 294920 | tf_op jit(solution)/shard_map/ppermute | solution.py:215
  9.2 1.0 %collective-permute-start.2 = (f32[2,6,4,512]{3,2,1,0:T(4,128)S(1)}, f32[2,6,4,512]{3,2,1,0:T(4,128)S(1)}, u32[]{:S(2)}, u32[]{:S(2)}) collective-permute-start(f32[2,6,4,512]{3,2,1,0:T(4,128)S(1)} %get-tuple-element.16), channel_id=1, source_target_pairs={{0,32},{16,48},{32,0},{48,16},{1,33},{17,49},{33,1},{49,17},{2,34}... | collective-permute-start | bytes 294920 | tf_op jit(solution)/shard_map/ppermute | solution.py:215
  10.2 2.8 %collective-permute-start.1 = (f32[2,6,4,512]{3,2,1,0:T(4,128)S(1)}, f32[2,6,4,512]{3,2,1,0:T(4,128)S(1)}, u32[]{:S(2)}, u32[]{:S(2)}) collective-permute-start(f32[2,6,4,512]{3,2,1,0:T(4,128)S(1)} %get-tuple-element.17), channel_id=1, source_target_pairs={{0,16},{16,32},{32,48},{48,0},{1,17},{17,33},{33,49},{49,1},{2,18}... | collective-permute-start | bytes 294920 | tf_op jit(solution)/shard_map/ppermute | solution.py:215
  13.0 3.0 %collective-permute-start.4 = (f32[2,6,4,512]{3,2,1,0:T(4,128)S(1)}, f32[2,6,4,512]{3,2,1,0:T(4,128)S(1)}, u32[]{:S(2)}, u32[]{:S(2)}) collective-permute-start(f32[2,6,4,512]{3,2,1,0:T(4,128)S(1)} %get-tuple-element.18.refs_0_), channel_id=1, source_target_pairs={{0,192},{16,208},{32,96},{48,112},{64,0},{80,16},{96,160},{112,176... | collective-permute-start | bytes 294920 | tf_op jit(solution)/shard_map/ppermute | solution.py:217
  16.1 1.9 %collective-permute-done.3.refs_3_ = f32[2,6,4,512]{3,2,1,0:T(4,128)S(1)} collective-permute-done((f32[2,6,4,512]{3,2,1,0:T(4,128)S(1)}, f32[2,6,4,512]{3,2,1,0:T(4,128)S(1)}, u32[]{:S(2)}, u32[]{:S(2)}) %collective-permute-start.3) | collective-permute-done | bytes 98336 | tf_op jit(solution)/shard_map/ppermute | solution.py:215
  17.9 3.0 %collective-permute-start.7 = (f32[2,6,4,512]{3,2,1,0:T(4,128)S(1)}, f32[2,6,4,512]{3,2,1,0:T(4,128)S(1)}, u32[]{:S(2)}, u32[]{:S(2)}) collective-permute-start(f32[2,6,4,512]{3,2,1,0:T(4,128)S(1)} %collective-permute-done.3.refs_3_), channel_id=1, source_target_pairs={{0,192},{16,80},{32,96},{48,240},{64,0},{80,144},{96,160},{112,48}... | collective-permute-start | bytes 294920 | tf_op jit(solution)/shard_map/ppermute | solution.py:217
  21.0 0.5 collective-permute-done.2.refs_2_
  21.5 1.6 %collective-permute-start.6 = (f32[2,6,4,512]{3,2,1,0:T(4,128)S(1)}, f32[2,6,4,512]{3,2,1,0:T(4,128)S(1)}, u32[]{:S(2)}, u32[]{:S(2)}) collective-permute-start(f32[2,6,4,512]{3,2,1,0:T(4,128)S(1)} %collective-permute-done.2.refs_2_), channel_id=1, source_target_pairs={{0,64},{16,80},{32,224},{48,240},{64,128},{80,144},{96,32},{112,48... | collective-permute-start | bytes 294920 | tf_op jit(solution)/shard_map/ppermute | solution.py:217
  23.0 0.0 collective-permute-done.1.refs_1_
  23.0 1.6 %collective-permute-start.5 = (f32[2,6,4,512]{3,2,1,0:T(4,128)S(1)}, f32[2,6,4,512]{3,2,1,0:T(4,128)S(1)}, u32[]{:S(2)}, u32[]{:S(2)}) collective-permute-start(f32[2,6,4,512]{3,2,1,0:T(4,128)S(1)} %collective-permute-done.1.refs_1_), channel_id=1, source_target_pairs={{0,64},{16,208},{32,224},{48,112},{64,128},{80,16},{96,32},{112,17... | collective-permute-start | bytes 294920 | tf_op jit(solution)/shard_map/ppermute | solution.py:217
  24.6 0.0 collective-permute-done.4.refs_4_
  24.6 0.0 collective-permute-done.7.refs_7_
  24.6 2.7 %collective-permute-done.6.refs_6_ = f32[2,6,4,512]{3,2,1,0:T(4,128)S(1)} collective-permute-done((f32[2,6,4,512]{3,2,1,0:T(4,128)S(1)}, f32[2,6,4,512]{3,2,1,0:T(4,128)S(1)}, u32[]{:S(2)}, u32[]{:S(2)}) %collective-permute-start.6) | collective-permute-done | bytes 98336 | tf_op jit(solution)/shard_map/ppermute | solution.py:217
  27.3 1.6 %collective-permute-done.5.refs_5_ = f32[2,6,4,512]{3,2,1,0:T(4,128)S(1)} collective-permute-done((f32[2,6,4,512]{3,2,1,0:T(4,128)S(1)}, f32[2,6,4,512]{3,2,1,0:T(4,128)S(1)}, u32[]{:S(2)}, u32[]{:S(2)}) %collective-permute-start.5) | collective-permute-done | bytes 98336 | tf_op jit(solution)/shard_map/ppermute | solution.py:217
  28.9 0.0 copy-done.1
  28.9 0.0 copy-done
  28.9 3.0 %filter.1 = f32[2,320,128]{2,1,0:T(8,128)S(1)} custom-call(f32[2,6,4,512]{3,2,1,0:T(4,128)S(1)} %get-tuple-element.18.refs_0_, f32[2,6,4,512]{3,2,1,0:T(4,128)S(1)} %collective-permute-done.1.refs_1_, f32[2,6,4,512]{3,2,1,0:T(4,128)S(1)} %collective-permute-done.2.refs_2_, f32[2,6,4,512]{3,2,1,0:T(4,128)S(1)} %collective-permute-done.3.refs_3_, ...), custom_call_target="tpu_custom_call" | custom-call | tf_op jit(solution)/shard_map/filter/pallas_call | solution.py:100
  31.8 0.0 copy-start.2
  31.9 0.1 collective-permute-start.8
  32.0 0.9 %copy-done.2 = f32[320,320]{1,0:T(8,128)S(1)} copy-done((f32[320,320]{1,0:T(8,128)S(1)}, f32[320,320]{1,0:T(8,128)}, u32[]{:S(2)}) %copy-start.2) | copy-done | bytes 409624
  32.9 0.2 turn.1
  33.1 0.3 collective-permute-done.8.got_ref
  33.4 19.5 %all_to_all.10 = f32[32,5,4,128]{3,2,1,0:T(4,128)S(1)} all-to-all(f32[32,5,4,128]{3,2,1,0:T(4,128)S(1)} %bitcast.31), channel_id=1, replica_groups=mesh['y'=4,'zh'=4,'core'=2,'x'=4,'zl'=2] {'x','zl','zh'}, dimensions={0} | all-to-all | bytes 655360 | tf_op jit(solution)/shard_map/all_to_all | solution.py:223
  52.9 0.4 rotate.1
  53.3 11.9 %all_to_all.11 = f32[8,40,256]{2,1,0:T(8,128)S(1)} all-to-all(f32[8,40,256]{2,1,0:T(8,128)S(1)} %bitcast.33), channel_id=1, replica_groups=mesh['y'=4,'zh'=4,'core'=2,'x'=4,'zl'=2] {'x','zl'}, dimensions={0} | all-to-all | bytes 655360 | tf_op jit(solution)/shard_map/all_to_all | solution.py:225
  65.2 0.2 copy.8
  65.4 1.0 %reshape.38 = f32[40,4,512]{2,1,0:T(4,128)} reshape(f32[40,4,2,256]{3,2,1,0:T(2,128)S(1)} %bitcast.35) | data formatting | bytes 655360 | tf_op jit(solution)/shard_map/reshape | solution.py:226
  (10 shorter events, 0.3 us)
Async XLA Ops:
  0.0 1.0 %copy-start.3 = (f32[4,512]{1,0:T(4,128)S(1)}, f32[4,512]{1,0:T(4,128)}, u32[]{:S(2)}) copy-start(f32[4,512]{1,0:T(4,128)} %param.6) | copy-start | bytes 24580
  1.1 1.5 %collective-permute-start = (f32[21,4,512]{2,1,0:T(4,128)S(1)}, f32[21,4,512]{2,1,0:T(4,128)S(1)}, u32[]{:S(2)}, u32[]{:S(2)}) collective-permute-start(f32[21,4,512]{2,1,0:T(4,128)S(1)} %pad_maximum_fusion), channel_id=1, source_target_pairs={{0,8},{8,0},{1,9},{9,1},{2,10},{10,2},{3,11},{11,3},{4,12},{12,4},... | collective-permute-start | bytes 516104 | tf_op jit(solution)/shard_map/ppermute | solution.py:197
  2.7 26.2 %copy-start.1 = (bf16[512,512]{1,0:T(8,128)(2,1)S(1)}, bf16[512,512]{1,0:T(8,128)(2,1)}, u32[]{:S(2)}) copy-start(bf16[512,512]{1,0:T(8,128)(2,1)} %constant.63.clone.refs_8_) | copy-start | bytes 1572868
  2.8 26.1 %copy-start = (bf16[512,512]{1,0:T(8,128)(2,1)S(1)}, bf16[512,512]{1,0:T(8,128)(2,1)}, u32[]{:S(2)}) copy-start(bf16[512,512]{1,0:T(8,128)(2,1)} %constant.64.clone.refs_9_) | copy-start | bytes 1572868
  2.9 15.1 %collective-permute-start.3 = (f32[2,6,4,512]{3,2,1,0:T(4,128)S(1)}, f32[2,6,4,512]{3,2,1,0:T(4,128)S(1)}, u32[]{:S(2)}, u32[]{:S(2)}) collective-permute-start(f32[2,6,4,512]{3,2,1,0:T(4,128)S(1)} %get-tuple-element.15), channel_id=1, source_target_pairs={{0,48},{16,0},{32,16},{48,32},{1,49},{17,1},{33,17},{49,33},{2,50}... | collective-permute-start | bytes 294920 | tf_op jit(solution)/shard_map/ppermute | solution.py:215
  9.2 12.2 %collective-permute-start.2 = (f32[2,6,4,512]{3,2,1,0:T(4,128)S(1)}, f32[2,6,4,512]{3,2,1,0:T(4,128)S(1)}, u32[]{:S(2)}, u32[]{:S(2)}) collective-permute-start(f32[2,6,4,512]{3,2,1,0:T(4,128)S(1)} %get-tuple-element.16), channel_id=1, source_target_pairs={{0,32},{16,48},{32,0},{48,16},{1,33},{17,49},{33,1},{49,17},{2,34}... | collective-permute-start | bytes 294920 | tf_op jit(solution)/shard_map/ppermute | solution.py:215
  10.2 12.8 %collective-permute-start.1 = (f32[2,6,4,512]{3,2,1,0:T(4,128)S(1)}, f32[2,6,4,512]{3,2,1,0:T(4,128)S(1)}, u32[]{:S(2)}, u32[]{:S(2)}) collective-permute-start(f32[2,6,4,512]{3,2,1,0:T(4,128)S(1)} %get-tuple-element.17), channel_id=1, source_target_pairs={{0,16},{16,32},{32,48},{48,0},{1,17},{17,33},{33,49},{49,1},{2,18}... | collective-permute-start | bytes 294920 | tf_op jit(solution)/shard_map/ppermute | solution.py:215
  13.0 11.6 %collective-permute-start.4 = (f32[2,6,4,512]{3,2,1,0:T(4,128)S(1)}, f32[2,6,4,512]{3,2,1,0:T(4,128)S(1)}, u32[]{:S(2)}, u32[]{:S(2)}) collective-permute-start(f32[2,6,4,512]{3,2,1,0:T(4,128)S(1)} %get-tuple-element.18.refs_0_), channel_id=1, source_target_pairs={{0,192},{16,208},{32,96},{48,112},{64,0},{80,16},{96,160},{112,176... | collective-permute-start | bytes 294920 | tf_op jit(solution)/shard_map/ppermute | solution.py:217
  17.9 6.7 %collective-permute-start.7 = (f32[2,6,4,512]{3,2,1,0:T(4,128)S(1)}, f32[2,6,4,512]{3,2,1,0:T(4,128)S(1)}, u32[]{:S(2)}, u32[]{:S(2)}) collective-permute-start(f32[2,6,4,512]{3,2,1,0:T(4,128)S(1)} %collective-permute-done.3.refs_3_), channel_id=1, source_target_pairs={{0,192},{16,80},{32,96},{48,240},{64,0},{80,144},{96,160},{112,48}... | collective-permute-start | bytes 294920 | tf_op jit(solution)/shard_map/ppermute | solution.py:217
  21.5 5.8 %collective-permute-start.6 = (f32[2,6,4,512]{3,2,1,0:T(4,128)S(1)}, f32[2,6,4,512]{3,2,1,0:T(4,128)S(1)}, u32[]{:S(2)}, u32[]{:S(2)}) collective-permute-start(f32[2,6,4,512]{3,2,1,0:T(4,128)S(1)} %collective-permute-done.2.refs_2_), channel_id=1, source_target_pairs={{0,64},{16,80},{32,224},{48,240},{64,128},{80,144},{96,32},{112,48... | collective-permute-start | bytes 294920 | tf_op jit(solution)/shard_map/ppermute | solution.py:217
  23.0 5.8 %collective-permute-start.5 = (f32[2,6,4,512]{3,2,1,0:T(4,128)S(1)}, f32[2,6,4,512]{3,2,1,0:T(4,128)S(1)}, u32[]{:S(2)}, u32[]{:S(2)}) collective-permute-start(f32[2,6,4,512]{3,2,1,0:T(4,128)S(1)} %collective-permute-done.1.refs_1_), channel_id=1, source_target_pairs={{0,64},{16,208},{32,224},{48,112},{64,128},{80,16},{96,32},{112,17... | collective-permute-start | bytes 294920 | tf_op jit(solution)/shard_map/ppermute | solution.py:217
  31.8 1.0 %copy-start.2 = (f32[320,320]{1,0:T(8,128)S(1)}, f32[320,320]{1,0:T(8,128)}, u32[]{:S(2)}) copy-start(f32[320,320]{1,0:T(8,128)} %weights_ref.1) | copy-start | bytes 1228804
  31.9 1.5 %collective-permute-start.8 = (f32[320,128]{1,0:T(8,128)S(1)}, f32[320,128]{1,0:T(8,128)S(1)}, u32[]{:S(2)}, u32[]{:S(2)}) collective-permute-start(f32[320,128]{1,0:T(8,128)S(1)} %get-tuple-element.20), channel_id=1, source_target_pairs={{0,8},{8,0},{1,9},{9,1},{2,10},{10,2},{3,11},{11,3},{4,12},{12,4},... | collective-permute-start | bytes 491528 | tf_op jit(solution)/shard_map/ppermute | solution.py:219

commit v2 on v1

v2 whole, which is shorter than its diff:
```python
import jax
import jax.numpy as jnp
import numpy as np
from jax import lax
from jax.experimental import pallas as pl
from jax.experimental.pallas import tpu as pltpu
from jax.sharding import Mesh
from jax.sharding import PartitionSpec as P


DEG = 4
NY = 16
NZ = 32
PLANE = NY * NZ
NORB = 320
BAND = ("x", "zl")
SPACE = ("y", "zh", "core")

coef_lap = (-205.0 / 72.0, 8.0 / 5.0, -1.0 / 5.0, 8.0 / 315.0, -1.0 / 560.0)
center_val = 6.0
half_width = 4.0
SCALE = -0.5 / half_width


def lateral():
    def ring(n):
        m = np.zeros((n, n))
        for k in range(1, 5):
            for i in range(n):
                m[i, (i + k) % n] += coef_lap[k]
                m[i, (i - k) % n] += coef_lap[k]
        return m

    lap = np.kron(np.eye(NY), ring(NZ)) + np.kron(ring(NY), np.eye(NZ))
    lap += 3.0 * coef_lap[0] * np.eye(PLANE)
    full = (SCALE * lap - (center_val / half_width) * np.eye(PLANE)).astype(np.float32)
    high = full.astype(jnp.bfloat16)
    low = (full - high.astype(np.float32)).astype(jnp.bfloat16)
    return high, low


def split(v):
    high = v.astype(jnp.bfloat16)
    low = (v - high.astype(jnp.float32)).astype(jnp.bfloat16)
    return high, low


def place(ref, at, buf_ref, pot_ref):
    rows = pl.ds(pl.multiple_of(at, 8), 8)
    for q in range(6):
        for j in range(4):
            part = jnp.concatenate(
                [ref[s, q, :, j * 128 : (j + 1) * 128] for s in range(2)], axis=0
            )
            if q < 5:
                buf_ref[q, j, rows, :] = part
            else:
                pot_ref[j, rows, :] = part * (1.0 / half_width)


def advance(spans, cur, prev, pot_ref, pot_at, mh_ref, ml_ref, emit):
    tall = sum(count for _, count in spans) * 5
    lanes = []
    for j in range(4):
        parts = [cur[q, j, 4 + at : 4 + at + n, :] for q in range(5) for at, n in spans]
        lanes.append(jnp.concatenate(parts, axis=0))
    high, low = split(jnp.concatenate(lanes, axis=1))
    dot = lambda a, b: jnp.dot(a, b, preferred_element_type=jnp.float32)
    lat = dot(high, mh_ref[...]) + (dot(low, mh_ref[...]) + dot(high, ml_ref[...]))
    row = 0
    for q in range(5):
        for at, n in spans:
            for j in range(4):
                acc = lat[row : row + n, j * 128 : (j + 1) * 128]
                acc = acc + pot_ref[j, pot_at + at : pot_at + at + n, :] * lanes[j][row : row + n]
                for k in range(1, 5):
                    acc = acc + (SCALE * coef_lap[k]) * (
                        cur[q, j, 4 + at + k : 4 + at + k + n, :]
                        + cur[q, j, 4 + at - k : 4 + at - k + n, :]
                    )
                if prev is not None:
                    acc = 2.0 * acc - prev[q, j, 8 + at : 8 + at + n, :]
                emit(q, j, at, n, acc)
            row += n
    assert row == tall


def saver(ref):
    def emit(q, j, at, n, acc):
        ref[q, j, at : at + n, :] = acc

    return emit


def inner_kernel(*refs):
    mh_ref, ml_ref, pot_ref = refs[4:7]
    levels = refs[7:11]
    zh_here = lax.axis_index("zh")
    for ahead in range(4):
        place(refs[ahead], lax.rem(zh_here + (4 - ahead), 4) * 8, levels[0], pot_ref)
    for step in range(1, DEG):
        prev = levels[step - 2] if step > 1 else None
        spans = ((0, 32 - 8 * step),)
        advance(
            spans, levels[step - 1], prev, pot_ref, 4 * step, mh_ref, ml_ref, saver(levels[step])
        )


def outer_kernel(*refs):
    halos, mh_ref, ml_ref, own_pot = refs[0:4], *refs[4:7]
    inner, out_ref, pot_ref = refs[7:11], refs[11], refs[12]
    levels = refs[13:17]
    zh_here = lax.axis_index("zh")
    for ahead in range(4):
        zh = lax.rem(zh_here + (4 - ahead), 4)
        place(halos[ahead], jnp.where(zh >= 2, (zh - 2) * 8, 48 + zh * 8), levels[0], pot_ref)
    pot_ref[:, 16:48, :] = own_pot[...]
    for step in range(DEG):
        levels[step][:, :, 16 : 48 - 8 * step, :] = inner[step][...]

    def emit(q, j, at, n, acc):
        half, tile = divmod(j, 2)
        for plane in range(at, at + n, 4):
            zh, s = divmod(plane // 4, 2)
            row = ((half * 4 + zh) * 2 + s) * 10 + q * 2 + tile
            out_ref[pl.ds(row, 4, stride=160), :] = acc[plane - at : plane - at + 4, :]

    for step in range(1, DEG + 1):
        prev = levels[step - 2] if step > 1 else None
        spans = ((0, 16), (48 - 8 * step, 16))
        advance(
            spans,
            levels[step - 1],
            prev,
            pot_ref,
            4 * step,
            mh_ref,
            ml_ref,
            emit if step == DEG else saver(levels[step]),
        )


def stack_of(rows):
    return (5, 4, rows, 128)


def run_inner(pieces, lat):
    vmem = pl.BlockSpec(memory_space=pltpu.VMEM)
    shapes = [(4, 32, 128)] + [stack_of(32 - 8 * s) for s in range(DEG)]
    return pl.pallas_call(
        inner_kernel,
        out_shape=[jax.ShapeDtypeStruct(shape, jnp.float32) for shape in shapes],
        in_specs=[vmem] * 6,
        out_specs=[vmem] * 5,
        compiler_params=pltpu.CompilerParams(vmem_limit_bytes=16 << 20),
        cost_estimate=pl.CostEstimate(flops=2 << 30, bytes_accessed=4 << 20, transcendentals=0),
        name="inner",
    )(*pieces, *lat)


def run_outer(halos, lat, found):
    vmem = pl.BlockSpec(memory_space=pltpu.VMEM)
    return pl.pallas_call(
        outer_kernel,
        out_shape=jax.ShapeDtypeStruct((640, 128), jnp.float32),
        in_specs=[vmem] * 11,
        out_specs=vmem,
        scratch_shapes=[pltpu.VMEM((4, 64, 128), jnp.float32)]
        + [pltpu.VMEM(stack_of(64 - 8 * s), jnp.float32) for s in range(DEG)],
        compiler_params=pltpu.CompilerParams(vmem_limit_bytes=20 << 20),
        name="outer",
    )(*halos, *lat, *found)


def turn_kernel(weights_ref, high_ref, low_ref):
    high_ref[...], low_ref[...] = split(weights_ref[...].T)


def run_turn(rotation):
    vmem = pl.BlockSpec(memory_space=pltpu.VMEM)
    return pl.pallas_call(
        turn_kernel,
        out_shape=[jax.ShapeDtypeStruct((NORB, NORB), jnp.bfloat16)] * 2,
        in_specs=[vmem],
        out_specs=[vmem] * 2,
        compiler_params=pltpu.CompilerParams(vmem_limit_bytes=8 << 20),
        name="turn",
    )(rotation)


def rotate_kernel(wh_ref, wl_ref, field_ref, out_ref):
    field = jnp.concatenate(
        [field_ref[pl.ds(tile, NORB, stride=2), :] for tile in range(2)], axis=1
    )
    high, low = split(field)
    dot = lambda a, b: jnp.dot(a, b, preferred_element_type=jnp.float32)
    wh = wh_ref[...]
    out_ref[...] = dot(wh, high) + (dot(wh, low) + dot(wl_ref[...], high))


def run_rotate(weights, field):
    vmem = pl.BlockSpec(memory_space=pltpu.VMEM)
    return pl.pallas_call(
        rotate_kernel,
        out_shape=jax.ShapeDtypeStruct((NORB, 256), jnp.float32),
        in_specs=[vmem] * 3,
        out_specs=vmem,
        compiler_params=pltpu.CompilerParams(vmem_limit_bytes=8 << 20),
        name="rotate",
    )(*weights, field)


SWAP = [(0, 1), (1, 0)]


def ahead_by(step):
    return [(zh, (zh + step) % 4) for zh in range(4)]


def outward(ahead):
    pairs = []
    for y in range(4):
        for zh in range(4):
            way = 1 if (zh - ahead) % 4 >= 2 else -1
            pairs.append((y * 4 + zh, (y + way) % 4 * 4 + zh))
    return pairs


def local(orbitals, potential, rotation):
    core, zh_here = lax.axis_index("core"), lax.axis_index("zh")
    pairs = orbitals.reshape(4, 2, 5, 4, PLANE)
    give = lax.dynamic_index_in_dim(pairs, 1 - core, 1, keepdims=False).reshape(20, 4, PLANE)
    keep = lax.dynamic_index_in_dim(pairs, core, 1, keepdims=False)
    give = jnp.concatenate([give, potential[None]], axis=0)
    got = lax.ppermute(give, "core", SWAP)

    def six(block, pot):
        block = block.reshape(4, 5, 4, PLANE)
        return jnp.concatenate(
            [block, jnp.broadcast_to(pot[None, None], (4, 1, 4, PLANE))], axis=1
        )

    own = six(keep, potential)
    other = six(got[:20], got[20])
    payload = jnp.where(
        core == 0,
        jnp.stack([own, other], axis=1),
        jnp.stack([other, own], axis=1),
    )
    pieces, halos = [None] * 4, [None] * 4
    for ahead in (2, 1, 3, 0):
        piece = lax.dynamic_index_in_dim(payload, (zh_here + ahead) % 4, 0, keepdims=False)
        pieces[ahead] = lax.ppermute(piece, "zh", ahead_by(ahead)) if ahead else piece
    for ahead in (0, 2, 1, 3):
        halos[ahead] = lax.ppermute(pieces[ahead], ("y", "zh"), outward(ahead))
    lat = tuple(jnp.asarray(part) for part in lateral())
    found = run_inner(pieces, lat)
    filtered = run_outer(halos, lat, found)
    weights = run_turn(rotation)
    filtered, weights = lax.optimization_barrier((filtered, weights))
    columns = lax.all_to_all(
        filtered.reshape(64, 5, 2, 128), BAND + ("zh", "core"), 0, 0, tiled=True
    )
    turned = run_rotate(weights, columns.reshape(640, 128))
    back = lax.all_to_all(turned.reshape(8, 40, 256), BAND, 0, 0, tiled=True)
    return back.reshape(4, 2, 40, 256).transpose(2, 0, 1, 3).reshape(40, 4, PLANE)


def solution(mesh):
    fine = Mesh(mesh.devices.reshape(4, 4, 2, 4, 2), SPACE + BAND)
    placed = (P(BAND, SPACE, None), P(SPACE, None), P())
    return jax.shard_map(
        local, mesh=fine, in_specs=placed, out_specs=P(BAND, SPACE, None), check_vma=False
    )
```

time: 66.8 us -> 65.9 us (0.987)
  waiting for transfers between devices: 8.16 us -> 4.33 us
  blocking collectives: 31.4 us -> 34.3 us
  local copies, waits for them, and re-layouts: 3.24 us -> 2.33 us
    all_to_all x1, blocking collectives: 19.5 us -> 23.2 us  [local(): lax.all_to_all(filtered.reshape(64, 5, 2, 128), BAND + ('zh', 'core'), 0,...]
    ppermute x4, waiting for transfers between devices: 4.25 us -> 0.95 us  [local(): halos[ahead] = lax.ppermute(pieces[ahead], ('y', 'zh'), outward(ahead))]
    ppermute x4, starting transfers between devices: 9.18 us -> 7.68 us  [local(): halos[ahead] = lax.ppermute(pieces[ahead], ('y', 'zh'), outward(ahead))]
    ppermute x3, starting transfers between devices: 10.2 us -> 11.4 us  [local(): lax.ppermute(piece, 'zh', ahead_by(ahead))]
    dynamic_slice x1 -> x0, local copies, waits for them, and re-layouts: 1.03 us -> none  [local(): keep = lax.dynamic_index_in_dim(pairs, core, 1, keepdims=False)]
    squeeze x1, local copies, waits for them, and re-layouts: 0.02 us -> 1.03 us  [local(): keep = lax.dynamic_index_in_dim(pairs, core, 1, keepdims=False)]
    unnamed x8, local copies, waits for them, and re-layouts: 0.91 us -> 0.02 us
    all_to_all x1, blocking collectives: 11.9 us -> 11.2 us  [local(): back = lax.all_to_all(turned.reshape(8, 40, 256), BAND, 0, 0, tiled=True)]
  transfers between devices with their start and end apart: 9 -> 8, of which waited for: 6 -> 4; matrix products, arithmetic and copies ran while one was open for 0% -> 0% of each run, Pallas kernels for 0% -> 2%
where the time goes in v2:
time: 65.9 us; the launch traced here: 64.9 us
  blocking collectives  34.3 us (52%)
  starting transfers between devices  19.2 us (29%)
  waiting for transfers between devices  4.33 us (7%)
  Pallas kernels  4.22 us (6%)
  local copies, waits for them, and re-layouts  2.33 us (4%)
    all_to_all x1, blocking collectives, local(): lax.all_to_all(filtered.reshape(64, 5, 2, 128), BAND + ('zh', 'core'), 0,...  23.2 us
    ppermute x3, starting transfers between devices, local(): lax.ppermute(piece, 'zh', ahead_by(ahead))  11.4 us
    all_to_all x1, blocking collectives, local(): back = lax.all_to_all(turned.reshape(8, 40, 256), BAND, 0, 0, tiled=True)  11.2 us
    ppermute x4, starting transfers between devices, local(): halos[ahead] = lax.ppermute(pieces[ahead], ('y', 'zh'), outward(ahead))  7.68 us
    pallas_call x1, Pallas kernels, run_outer(): pl.pallas_call(outer_kernel, out_shape=jax.ShapeDtypeStruct((640, 128), j...  2.35 us
    ppermute x3, waiting for transfers between devices, local(): lax.ppermute(piece, 'zh', ahead_by(ahead))  2.13 us
  transfers between devices with their start and end apart: 8, of which 4 were waited for; matrix products, arithmetic and copies ran while one was open for 0% of the time, Pallas kernels for 2%

profile of v2, /device:TPU:2, one launch (start us, length us, event | category | flops | bytes accessed | tf_op | source)
XLA Modules:
  0.0 64.9 jit_solution(4611314052523686867)
XLA Ops:
  0.0 0.0 copy-start.3
  0.0 1.0 %dynamic-slice_bitcast_fusion = (f32[4,5,4,512]{3,2,1,0:T(4,128)S(1)}, f32[4,1,5,4,512]{4,3,2,1,0:T(4,128)S(1)}) fusion(f32[4,2,5,4,512]{4,3,2,1,0:T(4,128)} %bitcast.34, s32[]{:T(128)S(6)} %select_n.48, s32[]{:T(128)S(6)} %select_n.49), kind=kLoop, calls=%fused_computation.5 | loop fusion | bytes 655368 | tf_op jit(solution)/shard_map/jit(dynamic_index_in_dim)/squeeze | solution.py:233
  1.0 0.0 copy-done.3
  1.1 0.1 collective-permute-start
  1.3 1.3 %collective-permute-done = f32[21,4,512]{2,1,0:T(4,128)S(1)} collective-permute-done((f32[21,4,512]{2,1,0:T(4,128)S(1)}, f32[21,4,512]{2,1,0:T(4,128)S(1)}, u32[]{:S(2)}, u32[]{:S(2)}) %collective-permute-start) | collective-permute-done | bytes 172064 | tf_op jit(solution)/shard_map/ppermute | solution.py:235
  2.7 0.0 copy-start.2
  2.7 0.1 maximum_select_fusion
  2.8 0.0 copy-start
  2.8 0.0 copy-start.1
  2.9 3.3 %collective-permute-start.2 = (f32[2,6,4,512]{3,2,1,0:T(4,128)S(1)}, f32[2,6,4,512]{3,2,1,0:T(4,128)S(1)}, u32[]{:S(2)}, u32[]{:S(2)}) collective-permute-start(f32[2,6,4,512]{3,2,1,0:T(4,128)S(1)} %get-tuple-element.27), channel_id=1, source_target_pairs={{0,16},{16,32},{32,48},{48,0},{1,17},{17,33},{33,49},{49,1},{2,18}... | collective-permute-start | bytes 294920 | tf_op jit(solution)/shard_map/ppermute | solution.py:253
  6.2 5.4 %collective-permute-start.4 = (f32[2,6,4,512]{3,2,1,0:T(4,128)S(1)}, f32[2,6,4,512]{3,2,1,0:T(4,128)S(1)}, u32[]{:S(2)}, u32[]{:S(2)}) collective-permute-start(f32[2,6,4,512]{3,2,1,0:T(4,128)S(1)} %get-tuple-element.26), channel_id=1, source_target_pairs={{0,32},{16,48},{32,0},{48,16},{1,33},{17,49},{33,1},{49,17},{2,34}... | collective-permute-start | bytes 294920 | tf_op jit(solution)/shard_map/ppermute | solution.py:253
  11.6 2.7 %collective-permute-start.6 = (f32[2,6,4,512]{3,2,1,0:T(4,128)S(1)}, f32[2,6,4,512]{3,2,1,0:T(4,128)S(1)}, u32[]{:S(2)}, u32[]{:S(2)}) collective-permute-start(f32[2,6,4,512]{3,2,1,0:T(4,128)S(1)} %get-tuple-element.25), channel_id=1, source_target_pairs={{0,48},{16,0},{32,16},{48,32},{1,49},{17,1},{33,17},{49,33},{2,50}... | collective-permute-start | bytes 294920 | tf_op jit(solution)/shard_map/ppermute | solution.py:253
  14.3 0.0 copy-done.2
  14.3 0.2 turn.1
  14.5 3.1 %collective-permute-start.1 = (f32[2,6,4,512]{3,2,1,0:T(4,128)S(1)}, f32[2,6,4,512]{3,2,1,0:T(4,128)S(1)}, u32[]{:S(2)}, u32[]{:S(2)}) collective-permute-start(f32[2,6,4,512]{3,2,1,0:T(4,128)S(1)} %get-tuple-element.28.refs_0_), channel_id=1, source_target_pairs={{0,192},{16,208},{32,96},{48,112},{64,0},{80,16},{96,160},{112,176... | collective-permute-start | bytes 294920 | tf_op jit(solution)/shard_map/ppermute | solution.py:255
  17.6 0.0 collective-permute-done.2.refs_1_
  17.6 0.0 collective-permute-start.3
  17.6 1.1 %collective-permute-done.4.refs_2_ = f32[2,6,4,512]{3,2,1,0:T(4,128)S(1)} collective-permute-done((f32[2,6,4,512]{3,2,1,0:T(4,128)S(1)}, f32[2,6,4,512]{3,2,1,0:T(4,128)S(1)}, u32[]{:S(2)}, u32[]{:S(2)}) %collective-permute-start.4) | collective-permute-done | bytes 98336 | tf_op jit(solution)/shard_map/ppermute | solution.py:253
  18.7 1.6 %collective-permute-start.5 = (f32[2,6,4,512]{3,2,1,0:T(4,128)S(1)}, f32[2,6,4,512]{3,2,1,0:T(4,128)S(1)}, u32[]{:S(2)}, u32[]{:S(2)}) collective-permute-start(f32[2,6,4,512]{3,2,1,0:T(4,128)S(1)} %collective-permute-done.4.refs_2_), channel_id=1, source_target_pairs={{0,64},{16,80},{32,224},{48,240},{64,128},{80,144},{96,32},{112,48... | collective-permute-start | bytes 294920 | tf_op jit(solution)/shard_map/ppermute | solution.py:255
  20.3 1.0 %collective-permute-done.6.refs_3_ = f32[2,6,4,512]{3,2,1,0:T(4,128)S(1)} collective-permute-done((f32[2,6,4,512]{3,2,1,0:T(4,128)S(1)}, f32[2,6,4,512]{3,2,1,0:T(4,128)S(1)}, u32[]{:S(2)}, u32[]{:S(2)}) %collective-permute-start.6) | collective-permute-done | bytes 98336 | tf_op jit(solution)/shard_map/ppermute | solution.py:253
  21.3 3.0 %collective-permute-start.7 = (f32[2,6,4,512]{3,2,1,0:T(4,128)S(1)}, f32[2,6,4,512]{3,2,1,0:T(4,128)S(1)}, u32[]{:S(2)}, u32[]{:S(2)}) collective-permute-start(f32[2,6,4,512]{3,2,1,0:T(4,128)S(1)} %collective-permute-done.6.refs_3_), channel_id=1, source_target_pairs={{0,192},{16,80},{32,96},{48,240},{64,0},{80,144},{96,160},{112,48}... | collective-permute-start | bytes 294920 | tf_op jit(solution)/shard_map/ppermute | solution.py:255
  24.3 0.0 copy-done
  24.3 0.0 copy-done.1
  24.3 1.3 %inner.1 = (f32[4,32,128]{2,1,0:T(8,128)S(1)}, f32[5,4,32,128]{3,2,1,0:T(8,128)S(1)}, f32[5,4,24,128]{3,2,1,0:T(8,128)S(1)}, f32[5,4,16,128]{3,2,1,0:T(8,128)S(1)}, f32[5,4,8,128]{3,2,1,0:T(8,128)S(1)}) custom-call(f32[2,6,4,512]{3,2,1,0:T(4,128)S(1)} %get-tuple-element.28.refs_0_, f32[2,6,4,512]{3,2,1,0:T(4,128)S(1)} %collective-permute-done.2.refs_1_, ...), custom_call_target="tpu_custom_call" | custom-call | flops 2147483648 | bytes 4194304 | tf_op jit(solution)/shard_map/inner/pallas_call | solution.py:150
  25.6 0.0 collective-permute-done.1.refs_0_
  25.6 0.0 collective-permute-done.3.refs_1_
  25.6 0.0 collective-permute-done.5.refs_2_
  25.6 0.9 %collective-permute-done.7.refs_3_ = f32[2,6,4,512]{3,2,1,0:T(4,128)S(1)} collective-permute-done((f32[2,6,4,512]{3,2,1,0:T(4,128)S(1)}, f32[2,6,4,512]{3,2,1,0:T(4,128)S(1)}, u32[]{:S(2)}, u32[]{:S(2)}) %collective-permute-start.7) | collective-permute-done | bytes 98336 | tf_op jit(solution)/shard_map/ppermute | solution.py:255
  26.6 2.3 %outer.1 = f32[640,128]{1,0:T(8,128)S(1)} custom-call(f32[2,6,4,512]{3,2,1,0:T(4,128)S(1)} %collective-permute-done.1.refs_0_, f32[2,6,4,512]{3,2,1,0:T(4,128)S(1)} %collective-permute-done.3.refs_1_, f32[2,6,4,512]{3,2,1,0:T(4,128)S(1)} %collective-permute-done.5.refs_2_, f32[2,6,4,512]{3,2,1,0:T(4,128)S(1)} %collective-permute-done.7.refs_3_, ...), custom_call_target="tpu_custom_call" | custom-call | tf_op jit(solution)/shard_map/outer/pallas_call | solution.py:163
  28.9 23.2 %all_to_all.10 = f32[64,5,2,128]{3,2,1,0:T(2,128)S(1)} all-to-all(f32[64,5,2,128]{3,2,1,0:T(2,128)S(1)} %bitcast.29), channel_id=1, replica_groups=mesh['y'=4,'zh'=4,'core'=2,'x'=4,'zl'=2] {'x','zl','zh','core'}, dimensions={0} | all-to-all | bytes 655360 | tf_op jit(solution)/shard_map/all_to_all | solution.py:261
  52.1 0.4 rotate.1
  52.5 11.2 %all_to_all.11 = f32[8,40,256]{2,1,0:T(8,128)S(1)} all-to-all(f32[8,40,256]{2,1,0:T(8,128)S(1)} %bitcast.28), channel_id=1, replica_groups=mesh['y'=4,'zh'=4,'core'=2,'x'=4,'zl'=2] {'x','zl'}, dimensions={0} | all-to-all | bytes 655360 | tf_op jit(solution)/shard_map/all_to_all | solution.py:265
  63.7 0.2 copy.8
  63.8 1.0 %reshape.38 = f32[40,4,512]{2,1,0:T(4,128)} reshape(f32[40,4,2,256]{3,2,1,0:T(2,128)S(1)} %bitcast.31) | data formatting | bytes 655360 | tf_op jit(solution)/shard_map/reshape | solution.py:266
  (8 shorter events, 0.2 us)
Async XLA Ops:
  0.0 1.0 %copy-start.3 = (f32[4,512]{1,0:T(4,128)S(1)}, f32[4,512]{1,0:T(4,128)}, u32[]{:S(2)}) copy-start(f32[4,512]{1,0:T(4,128)} %param.6) | copy-start | bytes 24580
  1.1 1.5 %collective-permute-start = (f32[21,4,512]{2,1,0:T(4,128)S(1)}, f32[21,4,512]{2,1,0:T(4,128)S(1)}, u32[]{:S(2)}, u32[]{:S(2)}) collective-permute-start(f32[21,4,512]{2,1,0:T(4,128)S(1)} %pad_maximum_fusion), channel_id=1, source_target_pairs={{0,8},{8,0},{1,9},{9,1},{2,10},{10,2},{3,11},{11,3},{4,12},{12,4},... | collective-permute-start | bytes 516104 | tf_op jit(solution)/shard_map/ppermute | solution.py:235
  2.7 11.6 %copy-start.2 = (f32[320,320]{1,0:T(8,128)S(1)}, f32[320,320]{1,0:T(8,128)}, u32[]{:S(2)}) copy-start(f32[320,320]{1,0:T(8,128)} %weights_ref.1) | copy-start | bytes 1228804
  2.8 21.5 %copy-start = (bf16[512,512]{1,0:T(8,128)(2,1)S(1)}, bf16[512,512]{1,0:T(8,128)(2,1)}, u32[]{:S(2)}) copy-start(bf16[512,512]{1,0:T(8,128)(2,1)} %constant.63.clone.refs_4_) | copy-start | bytes 1572868
  2.8 21.5 %copy-start.1 = (bf16[512,512]{1,0:T(8,128)(2,1)S(1)}, bf16[512,512]{1,0:T(8,128)(2,1)}, u32[]{:S(2)}) copy-start(bf16[512,512]{1,0:T(8,128)(2,1)} %constant.64.clone.refs_5_) | copy-start | bytes 1572868
  2.9 14.7 %collective-permute-start.2 = (f32[2,6,4,512]{3,2,1,0:T(4,128)S(1)}, f32[2,6,4,512]{3,2,1,0:T(4,128)S(1)}, u32[]{:S(2)}, u32[]{:S(2)}) collective-permute-start(f32[2,6,4,512]{3,2,1,0:T(4,128)S(1)} %get-tuple-element.27), channel_id=1, source_target_pairs={{0,16},{16,32},{32,48},{48,0},{1,17},{17,33},{33,49},{49,1},{2,18}... | collective-permute-start | bytes 294920 | tf_op jit(solution)/shard_map/ppermute | solution.py:253
  6.2 12.5 %collective-permute-start.4 = (f32[2,6,4,512]{3,2,1,0:T(4,128)S(1)}, f32[2,6,4,512]{3,2,1,0:T(4,128)S(1)}, u32[]{:S(2)}, u32[]{:S(2)}) collective-permute-start(f32[2,6,4,512]{3,2,1,0:T(4,128)S(1)} %get-tuple-element.26), channel_id=1, source_target_pairs={{0,32},{16,48},{32,0},{48,16},{1,33},{17,49},{33,1},{49,17},{2,34}... | collective-permute-start | bytes 294920 | tf_op jit(solution)/shard_map/ppermute | solution.py:253
  11.6 9.7 %collective-permute-start.6 = (f32[2,6,4,512]{3,2,1,0:T(4,128)S(1)}, f32[2,6,4,512]{3,2,1,0:T(4,128)S(1)}, u32[]{:S(2)}, u32[]{:S(2)}) collective-permute-start(f32[2,6,4,512]{3,2,1,0:T(4,128)S(1)} %get-tuple-element.25), channel_id=1, source_target_pairs={{0,48},{16,0},{32,16},{48,32},{1,49},{17,1},{33,17},{49,33},{2,50}... | collective-permute-start | bytes 294920 | tf_op jit(solution)/shard_map/ppermute | solution.py:253
  14.5 11.1 %collective-permute-start.1 = (f32[2,6,4,512]{3,2,1,0:T(4,128)S(1)}, f32[2,6,4,512]{3,2,1,0:T(4,128)S(1)}, u32[]{:S(2)}, u32[]{:S(2)}) collective-permute-start(f32[2,6,4,512]{3,2,1,0:T(4,128)S(1)} %get-tuple-element.28.refs_0_), channel_id=1, source_target_pairs={{0,192},{16,208},{32,96},{48,112},{64,0},{80,16},{96,160},{112,176... | collective-permute-start | bytes 294920 | tf_op jit(solution)/shard_map/ppermute | solution.py:255
  17.6 8.0 %collective-permute-start.3 = (f32[2,6,4,512]{3,2,1,0:T(4,128)S(1)}, f32[2,6,4,512]{3,2,1,0:T(4,128)S(1)}, u32[]{:S(2)}, u32[]{:S(2)}) collective-permute-start(f32[2,6,4,512]{3,2,1,0:T(4,128)S(1)} %collective-permute-done.2.refs_1_), channel_id=1, source_target_pairs={{0,64},{16,208},{32,224},{48,112},{64,128},{80,16},{96,32},{112,17... | collective-permute-start | bytes 294920 | tf_op jit(solution)/shard_map/ppermute | solution.py:255
  18.7 6.9 %collective-permute-start.5 = (f32[2,6,4,512]{3,2,1,0:T(4,128)S(1)}, f32[2,6,4,512]{3,2,1,0:T(4,128)S(1)}, u32[]{:S(2)}, u32[]{:S(2)}) collective-permute-start(f32[2,6,4,512]{3,2,1,0:T(4,128)S(1)} %collective-permute-done.4.refs_2_), channel_id=1, source_target_pairs={{0,64},{16,80},{32,224},{48,240},{64,128},{80,144},{96,32},{112,48... | collective-permute-start | bytes 294920 | tf_op jit(solution)/shard_map/ppermute | solution.py:255
  21.3 5.2 %collective-permute-start.7 = (f32[2,6,4,512]{3,2,1,0:T(4,128)S(1)}, f32[2,6,4,512]{3,2,1,0:T(4,128)S(1)}, u32[]{:S(2)}, u32[]{:S(2)}) collective-permute-start(f32[2,6,4,512]{3,2,1,0:T(4,128)S(1)} %collective-permute-done.6.refs_3_), channel_id=1, source_target_pairs={{0,192},{16,80},{32,96},{48,240},{64,0},{80,144},{96,160},{112,48}... | collective-permute-start | bytes 294920 | tf_op jit(solution)/shard_map/ppermute | solution.py:255
